TPU v7x, 32 devices: a whole 2x2x4 slice. The times are simulated.
32 devices in a mesh: seq: 16 (over z, x, core), tp: 2 (over y).
Axes of the slice: x: 2, y: 2, z: 4, core: 2. Of those that a mesh axis runs over, the one named last changes fastest.
Arguments:
- tokens: bfloat16 [8192, 4096], P('seq'), may hold values from -6 to 6
- w_in: bfloat16 [4096, 3, 4096], P('seq', None, 'tp'), may hold values from -0.09375 to 0.09375
- short_taps: float32 [3, 3, 4096], P(None, None, 'tp'), may hold values from -3 to 3
- decay_rate: float32 [256, 16], P('tp'), may hold values from 1.2207031e-05 to 0.04, as said below
- residue: float32 [256, 16], P('tp'), may hold values from -4 to 4
- skip_gain: float32 [4096], P('tp'), may hold values from -4 to 4
- w_out: bfloat16 [4096, 4096], P('tp'), may hold values from -0.125 to 0.125
Outputs:
- mixed: bfloat16 [8192, 4096], P('seq', 'tp')
Inputs may be any that keep to these rules, and one draw needn't show every extreme that they name: `decay_rate`: every decay rate is positive.
All inputs are finite; a program needn't handle non-finite values.
Results may differ from a plain program's by a relative error of at most 0.0075.
Values may be sent and summed in bfloat16 or wider, within the bound.
A program may use at most 192 MiB of HBM per device.

v0:
```python
import jax
import jax.numpy as jnp
from jax import lax
from jax.sharding import PartitionSpec as P

SUB = 128


def passed_along(block, axis, distance):
    devices = range(lax.axis_size(axis))
    route = [(i - distance, i) for i in devices if i - distance in devices]
    return lax.ppermute(block, axis, route)


def prefix(value, axis, combine, identity):
    peers, here = (lax.axis_size(axis), lax.axis_index(axis))
    everything = jax.tree.map(lambda part: lax.all_gather(part, axis), value)
    start = jax.tree.map(
        lambda part, zero: jnp.broadcast_to(jnp.asarray(zero, part.dtype), part.shape),
        value,
        identity,
    )

    def step(k, before):
        reached = k < here
        new = combine(before, jax.tree.map(lambda part: part[k], everything))
        return jax.tree.map(lambda a, b: jnp.where(reached, a, b), new, before)

    return lax.fori_loop(0, peers, step, start)


def shards(tokens, w_in, short_taps, decay_rate, residue, skip_gain, w_out):
    count = tokens.shape[0]
    chans = w_in.shape[2]
    groups = decay_rate.shape[0]
    order = decay_rate.shape[1]
    width = chans // groups
    taps = short_taps.shape[0]
    highest = lax.Precision.HIGHEST
    piece = lax.all_gather(w_in, "seq", axis=0, tiled=True)
    summed = jnp.dot(
        tokens, piece.reshape(piece.shape[0], 3 * chans), preferred_element_type=jnp.float32
    )
    proj = summed.astype(jnp.bfloat16).reshape(count, 3, chans)
    before = passed_along(proj[count - (taps - 1) :], "seq", 1)
    padded = jnp.concatenate([before, proj], axis=0).astype(jnp.float32)
    filtered = jnp.zeros((count, 3, chans), jnp.float32)
    for tap in range(taps):
        filtered = filtered + short_taps[tap] * padded[taps - 1 - tap : taps - 1 - tap + count]
    query = filtered[:, 0]
    gated = filtered[:, 1] * filtered[:, 2]
    weight_mode = residue * jnp.sqrt(2.0 * decay_rate / order)
    offsets = jnp.arange(SUB, dtype=jnp.float32)
    kernel = jnp.einsum(
        "gm,gmd->gd",
        weight_mode,
        jnp.exp(-decay_rate[:, :, None] * offsets[None, None, :]),
        precision=highest,
    )
    lag = jnp.arange(SUB)[:, None] - jnp.arange(SUB)[None, :]
    toeplitz = jnp.where(lag[None] >= 0, kernel[:, jnp.maximum(lag, 0)], 0.0)
    enter = weight_mode[:, None, :] * jnp.exp(
        -decay_rate[:, None, :] * (offsets[None, :, None] + 1.0)
    )
    leave = jnp.exp(-decay_rate[:, :, None] * (SUB - 1.0 - offsets[None, None, :]))
    fade = jnp.exp(-decay_rate * SUB)[:, :, None]
    blocks = gated.reshape(count // SUB, SUB, groups, width)

    def advance(state, block):
        local = jnp.einsum("gij,jgc->igc", toeplitz, block, precision=highest)
        local = local + jnp.einsum("gim,gmc->igc", enter, state, precision=highest)
        state = fade * state + jnp.einsum("gmj,jgc->gmc", leave, block, precision=highest)
        return (state, local)

    final_state, local_out = lax.scan(
        advance, jnp.zeros((groups, order, width), jnp.float32), blocks
    )
    local_out = local_out.reshape(count, groups, width)

    def combine(earlier, later):
        return (earlier[0] * later[0], later[1] + later[0][:, :, None] * earlier[1])

    hop = jnp.exp(-decay_rate * count)
    _, entering = prefix(
        (hop, final_state), "seq", combine, (jnp.ones_like(hop), jnp.zeros_like(final_state))
    )
    positions = jnp.arange(count, dtype=jnp.float32)
    reach = weight_mode[:, None, :] * jnp.exp(
        -decay_rate[:, None, :] * (positions[None, :, None] + 1.0)
    )
    carried = jnp.einsum("gtm,gmc->tgc", reach, entering, precision=highest)
    conv = (local_out + carried).reshape(count, chans)
    mix = (query * (conv + skip_gain * gated)).astype(jnp.bfloat16)
    partial_value = jnp.dot(mix, w_out, preferred_element_type=jnp.float32)
    return lax.psum_scatter(
        partial_value.astype(jnp.bfloat16), "tp", scatter_dimension=1, tiled=True
    )


def solution(mesh):
    in_specs = (
        P("seq", None),
        P("seq", None, "tp"),
        P(None, None, "tp"),
        P("tp", None),
        P("tp", None),
        P("tp"),
        P("tp", None),
    )
    out_specs = P("seq", "tp")
    return jax.shard_map(shards, mesh=mesh, in_specs=in_specs, out_specs=out_specs, check_vma=False)
```

profile of v0, /device:TPU:0, one launch (start us, length us, event | category | flops | bytes accessed | tf_op | source)
XLA Modules:
  0.0 692.5 jit_solution(16612572888679851134)
XLA Ops:
  6.5 4.8 copy.46
  11.4 0.1 copy.49
  11.5 0.1 copy.67
  11.7 0.6 multiply_reduce_fusion
  12.4 54.7 %gather_fusion = f32[16384,128]{1,0:T(8,128)} fusion(f32[128,128]{0,1:T(8,128)S(1)} %copy.62, s32[16384]{0:T(1024)S(1)} %bitcast_clamp_fusion), kind=kCustom, calls=%fused_computation | custom fusion | bytes 16842752 | tf_op jit(solution)/shard_map/gather | solution.py:61
  67.2 9.4 %copy.50 = f32[128,128,128]{1,0,2:T(8,128)} copy(f32[128,128,128]{2,1,0:T(8,128)} %bitcast.89) | data formatting | bytes 16777216 | tf_op jit(solution)/shard_map/gather | solution.py:61
  76.6 8.3 %select_bitcast_fusion = f32[128,128,128]{2,1,0:T(8,128)} fusion(f32[128,128,128]{1,0,2:T(8,128)} %copy.50, pred[128,128]{1,0:T(8,128)(4,1)S(1)} %subtract_compare_fusion), kind=kLoop, calls=%fused_computation.30 | loop fusion | flops 2097152 | bytes 16793600 | tf_op jit(solution)/shard_map/jit(_where)/select_n | solution.py:61
  84.9 185.2 %all-gather.5.cloned.1.call-done = bf16[4096,3,2048]{0,2,1:T(8,128)(2,1)} async-done(((bf16[256,3,2048]{0,2,1:T(8,128)(2,1)}), bf16[4096,3,2048]{0,2,1:T(8,128)(2,1)}) %all-gather.5.cloned.1.call-update) | async-done | bytes 50331664 | tf_op jit(solution)/shard_map/all_gather | solution.py:40
  270.1 33.7 %convolution_convert_fusion = bf16[512,6144]{1,0:T(8,128)(2,1)} fusion(bf16[512,4096]{1,0:T(8,128)(2,1)} %param.11, bf16[4096,6144]{0,1:T(8,128)(2,1)} %bitcast.96), kind=kOutput, calls=%fused_computation.29 | convolution fusion | flops 25772949504 | bytes 60817408 | tf_op jit(solution)/shard_map/dot_general | solution.py:41
  303.8 0.9 slice.46
  304.8 2.3 collective-permute-start
  307.2 8.7 %copy.47 = bf16[512,6144]{0,1:T(8,128)(2,1)} copy(bf16[512,6144]{1,0:T(8,128)(2,1)} %convolution_convert_fusion) | data formatting | bytes 12582912 | tf_op jit(solution)/shard_map/convert_element_type | solution.py:44
  315.8 0.9 copy.48
  316.7 11.7 %maximum_convert_fusion = f32[514,3,2048]{0,2,1:T(8,128)} fusion(bf16[512,3,2048]{0,2,1:T(8,128)(2,1)} %bitcast.90, bf16[2,3,2048]{0,2,1:T(8,128)(2,1)S(1)} %copy.48), kind=kLoop, calls=%fused_computation.31 | loop fusion | flops 12632064 | bytes 18948096 | tf_op jit(solution)/shard_map/convert_element_type | solution.py:46
  328.4 17.5 %fusion.19 = f32[512,3,2048]{0,2,1:T(8,128)S(1)} fusion(f32[514,3,2048]{0,2,1:T(8,128)} %maximum_convert_fusion, f32[3,2048]{1,0:T(4,128)S(1)} %get-tuple-element.340, f32[3,2048]{1,0:T(4,128)S(1)} %get-tuple-element.341, f32[3,2048]{1,0:T(4,128)S(1)} %get-tuple-element.339), kind=kLoop, calls=%fused_computation.25 | loop fusion | flops 15728640 | bytes 50405376 | tf_op jit(solution)/shard_map/add | solution.py:49
  345.9 4.5 copy-done
  350.4 3.0 slice_multiply_fusion.3
  353.4 5.2 mul.180
  358.6 198.3 %while.30 = (s32[]{:T(128)}, f32[128,16,16]{1,2,0:T(8,128)S(1)}, f32[4,128,128,16]{1,0,3,2:T(4,128)}, f32[128,16,1]{1,0,2:T(8,128)S(1)}, f32[4,128,128,16]{1,0,3...) while((s32[]{:T(128)}, f32[128,16,16]{1,2,0:T(8,128)S(1)}, ...), condition=%wide.region_1.2_spmd.clone.clone.clone, body=%wide.region_0.1_spmd.clone.clone.clone.sunk | while | flops 504496128 | bytes 18252936 | solution.py:75
  358.6 3.3 constant_dynamic-slice_fusion.5
  362.0 15.4 %fusion.57 = f32[128,16,128]{2,1,0:T(8,128)S(1)} fusion(f32[128,128,16]{0,2,1:T(8,128)S(1)} %bitcast.86, f32[128,128,128]{2,1,0:T(8,128)} %get-tuple-element.468), kind=kOutput, calls=%fused_computation.59.clone.1 | convolution fusion | flops 402653184 | bytes 10485760 | tf_op jit(solution)/shard_map/while/body/eval_jaxpr/gij,jgc->igc/dot_general | solution.py:70
  377.3 2.4 convolution_add_fusion.2
  379.7 26.6 %dynamic_update_slice.8 = f32[4,128,128,16]{1,0,3,2:T(4,128)} dynamic-update-slice(f32[4,128,128,16]{1,0,3,2:T(4,128)} %get-tuple-element.453, f32[1,128,128,16]{1,0,3,2:T(1,128)} %bitcast.88, s32[]{:T(128)} %get-tuple-element.451, s32[]{:T(128)} %constant.52.clone.1..sunk.1, s32[]{:T(128)} %constant.52.clone.1..sunk.1, s32[]{:T(128)} %constant.52.clone.1..sunk.1) | dynamic-update-slice | bytes 2097156 | tf_op jit(solution)/shard_map/while/body/jit(dynamic_update_index_in_dim)/dynamic_update_slice | solution.py:75
  406.3 1.9 fusion.56
  408.2 3.3 constant_dynamic-slice_fusion.5
  411.5 15.4 %fusion.57 = f32[128,16,128]{2,1,0:T(8,128)S(1)} fusion(f32[128,128,16]{0,2,1:T(8,128)S(1)} %bitcast.86, f32[128,128,128]{2,1,0:T(8,128)} %get-tuple-element.468), kind=kOutput, calls=%fused_computation.59.clone.1 | convolution fusion | flops 402653184 | bytes 10485760 | tf_op jit(solution)/shard_map/while/body/eval_jaxpr/gij,jgc->igc/dot_general | solution.py:70
  426.9 2.4 convolution_add_fusion.2
  429.3 26.6 %dynamic_update_slice.8 = f32[4,128,128,16]{1,0,3,2:T(4,128)} dynamic-update-slice(f32[4,128,128,16]{1,0,3,2:T(4,128)} %get-tuple-element.453, f32[1,128,128,16]{1,0,3,2:T(1,128)} %bitcast.88, s32[]{:T(128)} %get-tuple-element.451, s32[]{:T(128)} %constant.52.clone.1..sunk.1, s32[]{:T(128)} %constant.52.clone.1..sunk.1, s32[]{:T(128)} %constant.52.clone.1..sunk.1) | dynamic-update-slice | bytes 2097156 | tf_op jit(solution)/shard_map/while/body/jit(dynamic_update_index_in_dim)/dynamic_update_slice | solution.py:75
  455.9 1.9 fusion.56
  457.8 3.3 constant_dynamic-slice_fusion.5
  461.1 15.4 %fusion.57 = f32[128,16,128]{2,1,0:T(8,128)S(1)} fusion(f32[128,128,16]{0,2,1:T(8,128)S(1)} %bitcast.86, f32[128,128,128]{2,1,0:T(8,128)} %get-tuple-element.468), kind=kOutput, calls=%fused_computation.59.clone.1 | convolution fusion | flops 402653184 | bytes 10485760 | tf_op jit(solution)/shard_map/while/body/eval_jaxpr/gij,jgc->igc/dot_general | solution.py:70
  476.5 2.4 convolution_add_fusion.2
  478.9 26.6 %dynamic_update_slice.8 = f32[4,128,128,16]{1,0,3,2:T(4,128)} dynamic-update-slice(f32[4,128,128,16]{1,0,3,2:T(4,128)} %get-tuple-element.453, f32[1,128,128,16]{1,0,3,2:T(1,128)} %bitcast.88, s32[]{:T(128)} %get-tuple-element.451, s32[]{:T(128)} %constant.52.clone.1..sunk.1, s32[]{:T(128)} %constant.52.clone.1..sunk.1, s32[]{:T(128)} %constant.52.clone.1..sunk.1) | dynamic-update-slice | bytes 2097156 | tf_op jit(solution)/shard_map/while/body/jit(dynamic_update_index_in_dim)/dynamic_update_slice | solution.py:75
  505.5 1.9 fusion.56
  507.4 3.3 constant_dynamic-slice_fusion.5
  510.7 15.4 %fusion.57 = f32[128,16,128]{2,1,0:T(8,128)S(1)} fusion(f32[128,128,16]{0,2,1:T(8,128)S(1)} %bitcast.86, f32[128,128,128]{2,1,0:T(8,128)} %get-tuple-element.468), kind=kOutput, calls=%fused_computation.59.clone.1 | convolution fusion | flops 402653184 | bytes 10485760 | tf_op jit(solution)/shard_map/while/body/eval_jaxpr/gij,jgc->igc/dot_general | solution.py:70
  526.1 2.4 convolution_add_fusion.2
  528.5 26.6 %dynamic_update_slice.8 = f32[4,128,128,16]{1,0,3,2:T(4,128)} dynamic-update-slice(f32[4,128,128,16]{1,0,3,2:T(4,128)} %get-tuple-element.453, f32[1,128,128,16]{1,0,3,2:T(1,128)} %bitcast.88, s32[]{:T(128)} %get-tuple-element.451, s32[]{:T(128)} %constant.52.clone.1..sunk.1, s32[]{:T(128)} %constant.52.clone.1..sunk.1, s32[]{:T(128)} %constant.52.clone.1..sunk.1) | dynamic-update-slice | bytes 2097156 | tf_op jit(solution)/shard_map/while/body/jit(dynamic_update_index_in_dim)/dynamic_update_slice | solution.py:75
  555.1 1.9 fusion.56
  557.0 1.1 copy.54
  558.2 23.8 %all-gather.1 = f32[2048,16]{1,0:T(8,128)S(1)} all-gather(f32[128,16]{1,0:T(8,128)S(1)} %get-tuple-element.342), channel_id=3, replica_groups=mesh['seq'=16,'tp'=2] {'seq'}, dimensions={0}, use_global_device_ids=true | all-gather | bytes 139264 | tf_op jit(solution)/shard_map/all_gather | solution.py:17
  582.0 0.3 copy.56
  582.3 5.7 reshape.75
  588.0 12.8 %all-gather.7.cloned.1.call-done = f32[2048,16,16]{0,2,1:T(8,128)} async-done(((f32[128,16,16]{0,2,1:T(8,128)}), f32[2048,16,16]{0,2,1:T(8,128)}) %all-gather.7.cloned.1.call-update) | async-done | bytes 2097168 | tf_op jit(solution)/shard_map/all_gather | solution.py:17
  600.8 2.0 copy.68
  602.8 3.9 while.29
  602.8 0.1 constant_dynamic-slice_fusion.4
  603.0 0.1 constant_dynamic-slice_fusion.4
  603.3 0.1 constant_dynamic-slice_fusion.4
  603.5 0.1 constant_dynamic-slice_fusion.4
  603.8 0.1 constant_dynamic-slice_fusion.4
  604.0 0.1 constant_dynamic-slice_fusion.4
  604.3 0.1 constant_dynamic-slice_fusion.4
  604.5 0.1 constant_dynamic-slice_fusion.4
  604.7 0.1 constant_dynamic-slice_fusion.4
  605.0 0.1 constant_dynamic-slice_fusion.4
  605.5 0.1 constant_dynamic-slice_fusion.4
  605.9 0.1 constant_dynamic-slice_fusion.4
  606.2 0.1 constant_dynamic-slice_fusion.4
  606.7 0.5 copy.58
  607.2 6.0 bitcast_add_fusion
  613.2 5.1 fusion.22
  618.3 14.0 %convolution_convert_fusion.1 = bf16[512,4096]{1,0:T(8,128)(2,1)} fusion(bf16[512,2048]{0,1:T(8,128)(2,1)S(1)} %fusion.22, bf16[2048,4096]{1,0:T(8,128)(2,1)} %param.17), kind=kOutput, calls=%fused_computation.32 | convolution fusion | flops 8592031744 | bytes 23068672 | tf_op jit(solution)/shard_map/dot_general | solution.py:94
  632.3 53.6 %reduce-scatter.2.cloned.1.call-done = bf16[512,2048]{1,0:T(8,128)(2,1)} async-done(((bf16[512,4096]{1,0:T(8,128)(2,1)}), bf16[512,2048]{1,0:T(8,128)(2,1)}) %reduce-scatter.2.cloned.1.call-update) | async-done | bytes 2097168 | tf_op jit(solution)/shard_map/reduce_scatter | solution.py:95
  (63 shorter events, 2.3 us)
Async XLA Ops:
  6.5 4.9 copy-start.2
  6.5 5.0 copy-start.4
  6.5 263.6 %all-gather.5.cloned.1.call-start = ((), (), s32[]{:S(2)}) async-start(), calls=%async_computation.1 | async-start | bytes 53477376 | tf_op jit(solution)/shard_map/all_gather | solution.py:40
  11.3 589.5 %all-gather.7.cloned.1.call-start = ((), (), s32[]{:S(2)}) async-start(), calls=%async_computation.3 | async-start | bytes 2228224 | tf_op jit(solution)/shard_map/all_gather | solution.py:17
  67.2 9.4 %copy-start.1 = (f32[3,3,2048]{2,1,0:T(4,128)S(1)}, f32[3,3,2048]{2,1,0:T(4,128)}, u32[]{:S(2)}) copy-start(f32[3,3,2048]{2,1,0:T(4,128)} %param.13) | copy-start | bytes 221188
  304.8 11.0 %collective-permute-start = (bf16[2,3,2048]{2,1,0:T(4,128)(2,1)S(1)}, bf16[2,3,2048]{2,1,0:T(4,128)(2,1)S(1)}, u32[]{:S(2)}, u32[]{:S(2)}) collective-permute-start(bf16[2,3,2048]{2,1,0:T(4,128)(2,1)S(1)} %slice.35), channel_id=1, source_target_pairs={{0,2},{2,4},{4,6},{6,8},{8,10},{10,12},{12,14},{14,16},{16,18},{18... | collective-permute-start | bytes 73736 | tf_op jit(solution)/shard_map/ppermute | solution.py:12
  345.9 4.5 copy-start
  558.1 127.8 %reduce-scatter.2.cloned.1.call-start = ((), (), s32[]{:S(2)}) async-start(), calls=%async_computation.2 | async-start | bytes 6291456 | tf_op jit(solution)/shard_map/reduce_scatter | solution.py:95
  607.2 6.0 copy-start.3
Sparse Core Ops, SparseCore 0:
  11.5 258.6 all-gather.4
  558.2 42.5 all-gather.6
  632.4 53.4 reduce-scatter.1
where the time goes:
time: 696 us; the launch traced here: 692 us
  waiting for transfers between devices  252 us (36%)
  local copies, waits for them, and re-layouts  220 us (32%)
  matrix products  132 us (19%)
  other arithmetic  47.8 us (7%)
  blocking collectives  23.8 us (3%)
  between operations  13.3 us (2%)
    all_gather x1, waiting for transfers between devices, shards(): piece = lax.all_gather(w_in, 'seq', axis=0, tiled=True)  185 us
    dynamic_update_slice x4, local copies, waits for them, and re-layouts, shards(): lax.scan(advance, jnp.zeros((groups, order, width), jnp.float32), blocks)  106 us
    gather x2, local copies, waits for them, and re-layouts, shards(): toeplitz = jnp.where(lag[None] >= 0, kernel[:, jnp.maximum(lag, 0)], 0.0)  64.1 us
    dot_general x4, matrix products, advance(): local = jnp.einsum('gij,jgc->igc', toeplitz, block, precision=highest)  61.5 us
    reduce_scatter x1, waiting for transfers between devices, shards(): lax.psum_scatter(partial_value.astype(jnp.bfloat16), 'tp', scatter_dimens...  53.6 us
    dot_general x1, matrix products, shards(): jnp.dot(tokens, piece.reshape(piece.shape[0], 3 * chans), preferred_eleme...  33.7 us
    all_gather x1, blocking collectives, prefix(): everything = jax.tree.map(lambda part: lax.all_gather(part, axis), value)  23.8 us
    add x1, other arithmetic, shards(): filtered + short_taps[tap] * padded[taps - 1 - tap:taps - 1 - tap + count]  17.5 us
  transfers between devices with their start and end apart: 4, of which 3 were waited for; matrix products, arithmetic and copies ran while one was open for 13% of the time, Pallas kernels for 0%

commit v1 on v0

--- a/solution.py
+++ b/solution.py
@@ -37,7 +37,12 @@
     width = chans // groups
     taps = short_taps.shape[0]
     highest = lax.Precision.HIGHEST
-    piece = lax.all_gather(w_in, "seq", axis=0, tiled=True)
+    ring = [w_in]
+    for hop_ in range(15):
+        ring.append(lax.ppermute(ring[-1], "seq", [(dev, (dev + 1) % 16) for dev in range(16)]))
+    piece = jnp.roll(
+        jnp.concatenate(ring[::-1], axis=0), (lax.axis_index("seq") + 1) * ring[0].shape[0], axis=0
+    )
     summed = jnp.dot(
         tokens, piece.reshape(piece.shape[0], 3 * chans), preferred_element_type=jnp.float32
     )

time: 696 us -> 1200 us (1.72)
  waiting for transfers between devices: 252 us -> 621 us
  local copies, waits for them, and re-layouts: 220 us -> 343 us
    ppermute x0 -> x15, waiting for transfers between devices: none -> 552 us  [shards(): lax.ppermute(ring[-1], 'seq', [(dev, (dev + 1) % 16) for dev in range(16)])]
    all_gather x1 -> x0, waiting for transfers between devices: 185 us -> none  [shards(): piece = lax.all_gather(w_in, 'seq', axis=0, tiled=True)]
    unnamed x15 -> x108, local copies, waits for them, and re-layouts: 11.8 us -> 108 us
    dynamic_slice x0 -> x1, local copies, waits for them, and re-layouts: none -> 33.7 us  [shards(): jnp.roll(jnp.concatenate(ring[::-1], axis=0), (lax.axis_index('seq') + 1)...]
  transfers between devices with their start and end apart: 4 -> 18, of which waited for: 3 -> 17; matrix products, arithmetic and copies ran while one was open for 13% -> 7% of each run, Pallas kernels for 0% -> 0%
where the time goes in v1:
time: 1200 us; the launch traced here: 1190 us
  waiting for transfers between devices  621 us (52%)
  local copies, waits for them, and re-layouts  343 us (29%)
  matrix products  132 us (11%)
  other arithmetic  49.8 us (4%)
  blocking collectives  26 us (2%)
  between operations  14.2 us (1%)
    ppermute x15, waiting for transfers between devices, shards(): lax.ppermute(ring[-1], 'seq', [(dev, (dev + 1) % 16) for dev in range(16)])  552 us
    unnamed x108, local copies, waits for them, and re-layouts  108 us
    dynamic_update_slice x4, local copies, waits for them, and re-layouts, shards(): lax.scan(advance, jnp.zeros((groups, order, width), jnp.float32), blocks)  106 us
    gather x2, local copies, waits for them, and re-layouts, shards(): toeplitz = jnp.where(lag[None] >= 0, kernel[:, jnp.maximum(lag, 0)], 0.0)  63.9 us
    dot_general x4, matrix products, advance(): local = jnp.einsum('gij,jgc->igc', toeplitz, block, precision=highest)  61.5 us
    reduce_scatter x1, waiting for transfers between devices, shards(): lax.psum_scatter(partial_value.astype(jnp.bfloat16), 'tp', scatter_dimens...  53.6 us
    dynamic_slice x1, local copies, waits for them, and re-layouts, shards(): jnp.roll(jnp.concatenate(ring[::-1], axis=0), (lax.axis_index('seq') + 1)...  33.7 us
    dot_general x1, matrix products, shards(): jnp.dot(tokens, piece.reshape(piece.shape[0], 3 * chans), preferred_eleme...  32.9 us
  transfers between devices with their start and end apart: 18, of which 17 were waited for; matrix products, arithmetic and copies ran while one was open for 7% of the time, Pallas kernels for 0%

profile of v1, /device:TPU:0, one launch (start us, length us, event | category | flops | bytes accessed | tf_op | source)
XLA Modules:
  0.0 1189.0 jit_solution(16856317648095894136)
XLA Ops:
  6.5 3.2 copy.46
  10.3 39.9 %collective-permute-done = bf16[256,3,2048]{0,2,1:T(8,128)(2,1)S(1)} collective-permute-done((bf16[256,3,2048]{0,2,1:T(8,128)(2,1)S(1)}, bf16[256,3,2048]{0,2,1:T(8,128)(2,1)S(1)}, u32[]{:S(2)}, u32[]{:S(2)}) %collective-permute-start) | collective-permute-done | bytes 3145760 | tf_op jit(solution)/shard_map/ppermute | solution.py:42
  51.8 39.4 %collective-permute-done.1 = bf16[256,3,2048]{0,2,1:T(8,128)(2,1)S(1)} collective-permute-done((bf16[256,3,2048]{0,2,1:T(8,128)(2,1)S(1)}, bf16[256,3,2048]{0,2,1:T(8,128)(2,1)S(1)}, u32[]{:S(2)}, u32[]{:S(2)}) %collective-permute-start.1) | collective-permute-done | bytes 3145760 | tf_op jit(solution)/shard_map/ppermute | solution.py:42
  92.8 39.4 %collective-permute-done.2 = bf16[256,3,2048]{0,2,1:T(8,128)(2,1)S(1)} collective-permute-done((bf16[256,3,2048]{0,2,1:T(8,128)(2,1)S(1)}, bf16[256,3,2048]{0,2,1:T(8,128)(2,1)S(1)}, u32[]{:S(2)}, u32[]{:S(2)}) %collective-permute-start.2) | collective-permute-done | bytes 3145760 | tf_op jit(solution)/shard_map/ppermute | solution.py:42
  133.8 39.4 %collective-permute-done.3 = bf16[256,3,2048]{0,2,1:T(8,128)(2,1)S(1)} collective-permute-done((bf16[256,3,2048]{0,2,1:T(8,128)(2,1)S(1)}, bf16[256,3,2048]{0,2,1:T(8,128)(2,1)S(1)}, u32[]{:S(2)}, u32[]{:S(2)}) %collective-permute-start.3) | collective-permute-done | bytes 3145760 | tf_op jit(solution)/shard_map/ppermute | solution.py:42
  174.9 39.4 %collective-permute-done.4 = bf16[256,3,2048]{0,2,1:T(8,128)(2,1)S(1)} collective-permute-done((bf16[256,3,2048]{0,2,1:T(8,128)(2,1)S(1)}, bf16[256,3,2048]{0,2,1:T(8,128)(2,1)S(1)}, u32[]{:S(2)}, u32[]{:S(2)}) %collective-permute-start.4) | collective-permute-done | bytes 3145760 | tf_op jit(solution)/shard_map/ppermute | solution.py:42
  215.9 39.4 %collective-permute-done.5 = bf16[256,3,2048]{0,2,1:T(8,128)(2,1)S(1)} collective-permute-done((bf16[256,3,2048]{0,2,1:T(8,128)(2,1)S(1)}, bf16[256,3,2048]{0,2,1:T(8,128)(2,1)S(1)}, u32[]{:S(2)}, u32[]{:S(2)}) %collective-permute-start.5) | collective-permute-done | bytes 3145760 | tf_op jit(solution)/shard_map/ppermute | solution.py:42
  257.0 39.4 %collective-permute-done.6 = bf16[256,3,2048]{0,2,1:T(8,128)(2,1)S(1)} collective-permute-done((bf16[256,3,2048]{0,2,1:T(8,128)(2,1)S(1)}, bf16[256,3,2048]{0,2,1:T(8,128)(2,1)S(1)}, u32[]{:S(2)}, u32[]{:S(2)}) %collective-permute-start.6) | collective-permute-done | bytes 3145760 | tf_op jit(solution)/shard_map/ppermute | solution.py:42
  298.0 39.4 %collective-permute-done.7 = bf16[256,3,2048]{0,2,1:T(8,128)(2,1)S(1)} collective-permute-done((bf16[256,3,2048]{0,2,1:T(8,128)(2,1)S(1)}, bf16[256,3,2048]{0,2,1:T(8,128)(2,1)S(1)}, u32[]{:S(2)}, u32[]{:S(2)}) %collective-permute-start.7) | collective-permute-done | bytes 3145760 | tf_op jit(solution)/shard_map/ppermute | solution.py:42
  339.1 39.4 %collective-permute-done.8 = bf16[256,3,2048]{0,2,1:T(8,128)(2,1)S(1)} collective-permute-done((bf16[256,3,2048]{0,2,1:T(8,128)(2,1)S(1)}, bf16[256,3,2048]{0,2,1:T(8,128)(2,1)S(1)}, u32[]{:S(2)}, u32[]{:S(2)}) %collective-permute-start.8) | collective-permute-done | bytes 3145760 | tf_op jit(solution)/shard_map/ppermute | solution.py:42
  380.1 39.4 %collective-permute-done.9 = bf16[256,3,2048]{0,2,1:T(8,128)(2,1)S(1)} collective-permute-done((bf16[256,3,2048]{0,2,1:T(8,128)(2,1)S(1)}, bf16[256,3,2048]{0,2,1:T(8,128)(2,1)S(1)}, u32[]{:S(2)}, u32[]{:S(2)}) %collective-permute-start.9) | collective-permute-done | bytes 3145760 | tf_op jit(solution)/shard_map/ppermute | solution.py:42
  421.3 39.4 %collective-permute-done.10 = bf16[256,3,2048]{0,2,1:T(8,128)(2,1)S(1)} collective-permute-done((bf16[256,3,2048]{0,2,1:T(8,128)(2,1)S(1)}, bf16[256,3,2048]{0,2,1:T(8,128)(2,1)S(1)}, u32[]{:S(2)}, u32[]{:S(2)}) %collective-permute-start.10) | collective-permute-done | bytes 3145760 | tf_op jit(solution)/shard_map/ppermute | solution.py:42
  462.4 39.4 %collective-permute-done.11 = bf16[256,3,2048]{0,2,1:T(8,128)(2,1)S(1)} collective-permute-done((bf16[256,3,2048]{0,2,1:T(8,128)(2,1)S(1)}, bf16[256,3,2048]{0,2,1:T(8,128)(2,1)S(1)}, u32[]{:S(2)}, u32[]{:S(2)}) %collective-permute-start.11) | collective-permute-done | bytes 3145760 | tf_op jit(solution)/shard_map/ppermute | solution.py:42
  503.4 39.4 %collective-permute-done.12 = bf16[256,3,2048]{0,2,1:T(8,128)(2,1)S(1)} collective-permute-done((bf16[256,3,2048]{0,2,1:T(8,128)(2,1)S(1)}, bf16[256,3,2048]{0,2,1:T(8,128)(2,1)S(1)}, u32[]{:S(2)}, u32[]{:S(2)}) %collective-permute-start.12) | collective-permute-done | bytes 3145760 | tf_op jit(solution)/shard_map/ppermute | solution.py:42
  544.4 39.5 %collective-permute-done.13 = bf16[256,3,2048]{0,2,1:T(8,128)(2,1)} collective-permute-done((bf16[256,3,2048]{0,2,1:T(8,128)(2,1)S(1)}, bf16[256,3,2048]{0,2,1:T(8,128)(2,1)}, u32[]{:S(2)}, u32[]{:S(2)}) %collective-permute-start.13) | collective-permute-done | bytes 3145760 | tf_op jit(solution)/shard_map/ppermute | solution.py:42
  587.6 54.5 %gather_fusion = f32[16384,128]{1,0:T(8,128)} fusion(f32[128,128]{0,1:T(8,128)S(1)} %copy.64, s32[16384]{0:T(1024)S(1)} %bitcast_clamp_fusion), kind=kCustom, calls=%fused_computation | custom fusion | bytes 16842752 | tf_op jit(solution)/shard_map/gather | solution.py:66
  642.1 9.4 copy.52
  651.6 8.6 select_bitcast_fusion
  660.2 4.0 constant_dynamic-update-slice_fusion.31
  664.1 4.0 constant_dynamic-update-slice_fusion.30
  695.0 3.8 constant_dynamic-update-slice_fusion.15
  698.8 3.9 constant_dynamic-update-slice_fusion.14
  702.7 3.9 constant_dynamic-update-slice_fusion.13
  706.6 3.8 constant_dynamic-update-slice_fusion.12
  712.4 2.0 constant_dynamic-update-slice_fusion.10
  714.4 2.0 constant_dynamic-update-slice_fusion.9
  718.4 2.0 constant_dynamic-update-slice_fusion.7
  724.3 2.0 constant_dynamic-update-slice_fusion.4
  726.2 2.0 constant_dynamic-update-slice_fusion.3
  732.1 2.0 constant_dynamic-update-slice_fusion
  734.1 33.7 %constant_dynamic-slice_fusion.2 = bf16[4096,3,2048]{0,2,1:T(8,128)(2,1)} fusion(bf16[8192,3,2048]{0,2,1:T(8,128)(2,1)} %constant_dynamic-update-slice_fusion, s32[]{:T(128)S(6)} %select_n.41), kind=kLoop, calls=%fused_computation.91 | loop fusion | bytes 100663296 | tf_op jit(solution)/shard_map/jit(_roll_dynamic)/dynamic_slice | solution.py:43
  767.8 32.9 %convolution_convert_fusion = bf16[6144,512]{1,0:T(8,128)(2,1)S(1)} fusion(bf16[4096,6144]{0,1:T(8,128)(2,1)} %bitcast.92, bf16[512,4096]{1,0:T(8,128)(2,1)} %param.11), kind=kOutput, calls=%fused_computation.29 | convolution fusion | flops 25772949504 | bytes 60817408 | tf_op jit(solution)/shard_map/dot_general | solution.py:46
  800.8 2.6 copy-done.27
  807.8 11.6 maximum_convert_fusion
  819.4 17.9 %fusion.19 = f32[512,3,2048]{0,2,1:T(8,128)S(1)} fusion(f32[514,3,2048]{0,2,1:T(8,128)} %maximum_convert_fusion, f32[3,2048]{1,0:T(4,128)S(1)} %get-tuple-element.340, f32[3,2048]{1,0:T(4,128)S(1)} %get-tuple-element.341, f32[3,2048]{1,0:T(4,128)S(1)} %get-tuple-element.339), kind=kLoop, calls=%fused_computation.25 | loop fusion | flops 15728640 | bytes 50405376 | tf_op jit(solution)/shard_map/add | solution.py:54
  837.4 4.6 copy-done
  842.0 3.0 slice_multiply_fusion.3
  845.0 5.2 mul.184
  850.2 198.5 %while.30 = (s32[]{:T(128)}, f32[128,16,16]{1,2,0:T(8,128)S(1)}, f32[4,128,128,16]{1,0,3,2:T(4,128)}, f32[128,16,1]{1,0,2:T(8,128)S(1)}, f32[4,128,128,16]{1,0,3...) while((s32[]{:T(128)}, f32[128,16,16]{1,2,0:T(8,128)S(1)}, ...), condition=%wide.region_1.2_spmd.clone.clone.clone, body=%wide.region_0.1_spmd.clone.clone.clone.sunk | while | flops 504496128 | bytes 18252936 | solution.py:80
  850.5 3.3 constant_dynamic-slice_fusion.6
  853.8 15.4 %fusion.57 = f32[128,16,128]{2,1,0:T(8,128)S(1)} fusion(f32[128,128,16]{0,2,1:T(8,128)S(1)} %bitcast.89, f32[128,128,128]{2,1,0:T(8,128)} %get-tuple-element.468), kind=kOutput, calls=%fused_computation.92.clone.1 | convolution fusion | flops 402653184 | bytes 10485760 | tf_op jit(solution)/shard_map/while/body/eval_jaxpr/gij,jgc->igc/dot_general | solution.py:75
  869.2 2.4 convolution_add_fusion.2
  871.6 26.5 %dynamic_update_slice.8 = f32[4,128,128,16]{1,0,3,2:T(4,128)} dynamic-update-slice(f32[4,128,128,16]{1,0,3,2:T(4,128)} %get-tuple-element.453, f32[1,128,128,16]{1,0,3,2:T(1,128)} %bitcast.91, s32[]{:T(128)} %get-tuple-element.451, s32[]{:T(128)} %constant.77.clone.1..sunk.1, s32[]{:T(128)} %constant.77.clone.1..sunk.1, s32[]{:T(128)} %constant.77.clone.1..sunk.1) | dynamic-update-slice | bytes 2097156 | tf_op jit(solution)/shard_map/while/body/jit(dynamic_update_index_in_dim)/dynamic_update_slice | solution.py:80
  900.0 3.3 constant_dynamic-slice_fusion.6
  903.4 15.4 %fusion.57 = f32[128,16,128]{2,1,0:T(8,128)S(1)} fusion(f32[128,128,16]{0,2,1:T(8,128)S(1)} %bitcast.89, f32[128,128,128]{2,1,0:T(8,128)} %get-tuple-element.468), kind=kOutput, calls=%fused_computation.92.clone.1 | convolution fusion | flops 402653184 | bytes 10485760 | tf_op jit(solution)/shard_map/while/body/eval_jaxpr/gij,jgc->igc/dot_general | solution.py:75
  918.7 2.4 convolution_add_fusion.2
  921.2 26.5 %dynamic_update_slice.8 = f32[4,128,128,16]{1,0,3,2:T(4,128)} dynamic-update-slice(f32[4,128,128,16]{1,0,3,2:T(4,128)} %get-tuple-element.453, f32[1,128,128,16]{1,0,3,2:T(1,128)} %bitcast.91, s32[]{:T(128)} %get-tuple-element.451, s32[]{:T(128)} %constant.77.clone.1..sunk.1, s32[]{:T(128)} %constant.77.clone.1..sunk.1, s32[]{:T(128)} %constant.77.clone.1..sunk.1) | dynamic-update-slice | bytes 2097156 | tf_op jit(solution)/shard_map/while/body/jit(dynamic_update_index_in_dim)/dynamic_update_slice | solution.py:80
  949.6 3.3 constant_dynamic-slice_fusion.6
  953.0 15.4 %fusion.57 = f32[128,16,128]{2,1,0:T(8,128)S(1)} fusion(f32[128,128,16]{0,2,1:T(8,128)S(1)} %bitcast.89, f32[128,128,128]{2,1,0:T(8,128)} %get-tuple-element.468), kind=kOutput, calls=%fused_computation.92.clone.1 | convolution fusion | flops 402653184 | bytes 10485760 | tf_op jit(solution)/shard_map/while/body/eval_jaxpr/gij,jgc->igc/dot_general | solution.py:75
  968.3 2.4 convolution_add_fusion.2
  970.7 26.5 %dynamic_update_slice.8 = f32[4,128,128,16]{1,0,3,2:T(4,128)} dynamic-update-slice(f32[4,128,128,16]{1,0,3,2:T(4,128)} %get-tuple-element.453, f32[1,128,128,16]{1,0,3,2:T(1,128)} %bitcast.91, s32[]{:T(128)} %get-tuple-element.451, s32[]{:T(128)} %constant.77.clone.1..sunk.1, s32[]{:T(128)} %constant.77.clone.1..sunk.1, s32[]{:T(128)} %constant.77.clone.1..sunk.1) | dynamic-update-slice | bytes 2097156 | tf_op jit(solution)/shard_map/while/body/jit(dynamic_update_index_in_dim)/dynamic_update_slice | solution.py:80
  999.2 3.3 constant_dynamic-slice_fusion.6
  1002.5 15.4 %fusion.57 = f32[128,16,128]{2,1,0:T(8,128)S(1)} fusion(f32[128,128,16]{0,2,1:T(8,128)S(1)} %bitcast.89, f32[128,128,128]{2,1,0:T(8,128)} %get-tuple-element.468), kind=kOutput, calls=%fused_computation.92.clone.1 | convolution fusion | flops 402653184 | bytes 10485760 | tf_op jit(solution)/shard_map/while/body/eval_jaxpr/gij,jgc->igc/dot_general | solution.py:75
  1017.9 2.4 convolution_add_fusion.2
  1020.3 26.5 %dynamic_update_slice.8 = f32[4,128,128,16]{1,0,3,2:T(4,128)} dynamic-update-slice(f32[4,128,128,16]{1,0,3,2:T(4,128)} %get-tuple-element.453, f32[1,128,128,16]{1,0,3,2:T(1,128)} %bitcast.91, s32[]{:T(128)} %get-tuple-element.451, s32[]{:T(128)} %constant.77.clone.1..sunk.1, s32[]{:T(128)} %constant.77.clone.1..sunk.1, s32[]{:T(128)} %constant.77.clone.1..sunk.1) | dynamic-update-slice | bytes 2097156 | tf_op jit(solution)/shard_map/while/body/jit(dynamic_update_index_in_dim)/dynamic_update_slice | solution.py:80
  1050.0 26.0 %all-gather.1 = f32[2048,16]{1,0:T(8,128)S(1)} all-gather(f32[128,16]{1,0:T(8,128)S(1)} %copy-done.33), channel_id=3, replica_groups=mesh['seq'=16,'tp'=2] {'seq'}, dimensions={0}, use_global_device_ids=true | all-gather | bytes 139264 | tf_op jit(solution)/shard_map/all_gather | solution.py:17
  1076.3 5.7 reshape.75
  1082.1 14.6 %all-gather.4.cloned.1.call-done = f32[2048,16,16]{0,2,1:T(8,128)} async-done(((f32[128,16,16]{0,2,1:T(8,128)}), f32[2048,16,16]{0,2,1:T(8,128)}) %all-gather.4.cloned.1.call-update) | async-done | bytes 2097168 | tf_op jit(solution)/shard_map/all_gather | solution.py:17
  1096.6 2.0 copy.70
  1098.6 3.9 while.29
  1103.0 6.0 bitcast_add_fusion
  1109.0 5.1 fusion.22
  1114.2 13.9 %convolution_convert_fusion.1 = bf16[512,4096]{1,0:T(8,128)(2,1)} fusion(bf16[512,2048]{0,1:T(8,128)(2,1)S(1)} %fusion.22, bf16[2048,4096]{1,0:T(8,128)(2,1)} %param.17), kind=kOutput, calls=%fused_computation.32 | convolution fusion | flops 8592031744 | bytes 23068672 | tf_op jit(solution)/shard_map/dot_general | solution.py:99
  1128.1 53.6 %reduce-scatter.2.cloned.1.call-done = bf16[512,2048]{1,0:T(8,128)(2,1)} async-done(((bf16[512,4096]{1,0:T(8,128)(2,1)}), bf16[512,2048]{1,0:T(8,128)(2,1)}) %reduce-scatter.2.cloned.1.call-update) | async-done | bytes 2097168 | tf_op jit(solution)/shard_map/reduce_scatter | solution.py:100
  (184 shorter events, 81.6 us)
Async XLA Ops:
  6.5 1090.1 %all-gather.4.cloned.1.call-start = ((), (), s32[]{:S(2)}) async-start(), calls=%async_computation.2 | async-start | bytes 2228224 | tf_op jit(solution)/shard_map/all_gather | solution.py:17
  9.7 40.5 %collective-permute-start = (bf16[256,3,2048]{0,2,1:T(8,128)(2,1)S(1)}, bf16[256,3,2048]{0,2,1:T(8,128)(2,1)S(1)}, u32[]{:S(2)}, u32[]{:S(2)}) collective-permute-start(bf16[256,3,2048]{0,2,1:T(8,128)(2,1)S(1)} %copy.46), channel_id=1, source_target_pairs={{0,2},{2,4},{4,6},{6,8},{8,10},{10,12},{12,14},{14,16},{16,18},{18... | collective-permute-start | bytes 9437192 | tf_op jit(solution)/shard_map/ppermute | solution.py:42
  50.2 1.6 copy-start.1
  51.8 39.4 %collective-permute-start.1 = (bf16[256,3,2048]{0,2,1:T(8,128)(2,1)S(1)}, bf16[256,3,2048]{0,2,1:T(8,128)(2,1)S(1)}, u32[]{:S(2)}, u32[]{:S(2)}) collective-permute-start(bf16[256,3,2048]{0,2,1:T(8,128)(2,1)S(1)} %collective-permute-done), channel_id=1, source_target_pairs={{0,2},{2,4},{4,6},{6,8},{8,10},{10,12},{12,14},{14,16},{16,18},{18... | collective-permute-start | bytes 9437192 | tf_op jit(solution)/shard_map/ppermute | solution.py:42
  91.2 1.6 copy-start.3
  92.8 39.4 %collective-permute-start.2 = (bf16[256,3,2048]{0,2,1:T(8,128)(2,1)S(1)}, bf16[256,3,2048]{0,2,1:T(8,128)(2,1)S(1)}, u32[]{:S(2)}, u32[]{:S(2)}) collective-permute-start(bf16[256,3,2048]{0,2,1:T(8,128)(2,1)S(1)} %collective-permute-done.1), channel_id=1, source_target_pairs={{0,2},{2,4},{4,6},{6,8},{8,10},{10,12},{12,14},{14,16},{16,18},{18... | collective-permute-start | bytes 9437192 | tf_op jit(solution)/shard_map/ppermute | solution.py:42
  132.2 1.6 copy-start.5
  133.8 39.4 %collective-permute-start.3 = (bf16[256,3,2048]{0,2,1:T(8,128)(2,1)S(1)}, bf16[256,3,2048]{0,2,1:T(8,128)(2,1)S(1)}, u32[]{:S(2)}, u32[]{:S(2)}) collective-permute-start(bf16[256,3,2048]{0,2,1:T(8,128)(2,1)S(1)} %collective-permute-done.2), channel_id=1, source_target_pairs={{0,2},{2,4},{4,6},{6,8},{8,10},{10,12},{12,14},{14,16},{16,18},{18... | collective-permute-start | bytes 9437192 | tf_op jit(solution)/shard_map/ppermute | solution.py:42
  173.2 1.7 copy-start.7
  174.9 39.4 %collective-permute-start.4 = (bf16[256,3,2048]{0,2,1:T(8,128)(2,1)S(1)}, bf16[256,3,2048]{0,2,1:T(8,128)(2,1)S(1)}, u32[]{:S(2)}, u32[]{:S(2)}) collective-permute-start(bf16[256,3,2048]{0,2,1:T(8,128)(2,1)S(1)} %collective-permute-done.3), channel_id=1, source_target_pairs={{0,2},{2,4},{4,6},{6,8},{8,10},{10,12},{12,14},{14,16},{16,18},{18... | collective-permute-start | bytes 9437192 | tf_op jit(solution)/shard_map/ppermute | solution.py:42
  214.3 1.6 copy-start.9
  215.9 39.4 %collective-permute-start.5 = (bf16[256,3,2048]{0,2,1:T(8,128)(2,1)S(1)}, bf16[256,3,2048]{0,2,1:T(8,128)(2,1)S(1)}, u32[]{:S(2)}, u32[]{:S(2)}) collective-permute-start(bf16[256,3,2048]{0,2,1:T(8,128)(2,1)S(1)} %collective-permute-done.4), channel_id=1, source_target_pairs={{0,2},{2,4},{4,6},{6,8},{8,10},{10,12},{12,14},{14,16},{16,18},{18... | collective-permute-start | bytes 9437192 | tf_op jit(solution)/shard_map/ppermute | solution.py:42
  255.3 1.7 copy-start.11
  257.0 39.4 %collective-permute-start.6 = (bf16[256,3,2048]{0,2,1:T(8,128)(2,1)S(1)}, bf16[256,3,2048]{0,2,1:T(8,128)(2,1)S(1)}, u32[]{:S(2)}, u32[]{:S(2)}) collective-permute-start(bf16[256,3,2048]{0,2,1:T(8,128)(2,1)S(1)} %collective-permute-done.5), channel_id=1, source_target_pairs={{0,2},{2,4},{4,6},{6,8},{8,10},{10,12},{12,14},{14,16},{16,18},{18... | collective-permute-start | bytes 9437192 | tf_op jit(solution)/shard_map/ppermute | solution.py:42
  296.3 1.6 copy-start.13
  298.0 39.4 %collective-permute-start.7 = (bf16[256,3,2048]{0,2,1:T(8,128)(2,1)S(1)}, bf16[256,3,2048]{0,2,1:T(8,128)(2,1)S(1)}, u32[]{:S(2)}, u32[]{:S(2)}) collective-permute-start(bf16[256,3,2048]{0,2,1:T(8,128)(2,1)S(1)} %collective-permute-done.6), channel_id=1, source_target_pairs={{0,2},{2,4},{4,6},{6,8},{8,10},{10,12},{12,14},{14,16},{16,18},{18... | collective-permute-start | bytes 9437192 | tf_op jit(solution)/shard_map/ppermute | solution.py:42
  337.4 1.7 copy-start.15
  339.1 39.4 %collective-permute-start.8 = (bf16[256,3,2048]{0,2,1:T(8,128)(2,1)S(1)}, bf16[256,3,2048]{0,2,1:T(8,128)(2,1)S(1)}, u32[]{:S(2)}, u32[]{:S(2)}) collective-permute-start(bf16[256,3,2048]{0,2,1:T(8,128)(2,1)S(1)} %collective-permute-done.7), channel_id=1, source_target_pairs={{0,2},{2,4},{4,6},{6,8},{8,10},{10,12},{12,14},{14,16},{16,18},{18... | collective-permute-start | bytes 9437192 | tf_op jit(solution)/shard_map/ppermute | solution.py:42
  378.4 1.7 copy-start.17
  380.1 39.4 %collective-permute-start.9 = (bf16[256,3,2048]{0,2,1:T(8,128)(2,1)S(1)}, bf16[256,3,2048]{0,2,1:T(8,128)(2,1)S(1)}, u32[]{:S(2)}, u32[]{:S(2)}) collective-permute-start(bf16[256,3,2048]{0,2,1:T(8,128)(2,1)S(1)} %collective-permute-done.8), channel_id=1, source_target_pairs={{0,2},{2,4},{4,6},{6,8},{8,10},{10,12},{12,14},{14,16},{16,18},{18... | collective-permute-start | bytes 9437192 | tf_op jit(solution)/shard_map/ppermute | solution.py:42
  419.5 1.8 copy-start.19
  421.3 39.4 %collective-permute-start.10 = (bf16[256,3,2048]{0,2,1:T(8,128)(2,1)S(1)}, bf16[256,3,2048]{0,2,1:T(8,128)(2,1)S(1)}, u32[]{:S(2)}, u32[]{:S(2)}) collective-permute-start(bf16[256,3,2048]{0,2,1:T(8,128)(2,1)S(1)} %collective-permute-done.9), channel_id=1, source_target_pairs={{0,2},{2,4},{4,6},{6,8},{8,10},{10,12},{12,14},{14,16},{16,18},{18... | collective-permute-start | bytes 9437192 | tf_op jit(solution)/shard_map/ppermute | solution.py:42
  460.6 1.7 copy-start.21
  462.4 39.4 %collective-permute-start.11 = (bf16[256,3,2048]{0,2,1:T(8,128)(2,1)S(1)}, bf16[256,3,2048]{0,2,1:T(8,128)(2,1)S(1)}, u32[]{:S(2)}, u32[]{:S(2)}) collective-permute-start(bf16[256,3,2048]{0,2,1:T(8,128)(2,1)S(1)} %collective-permute-done.10), channel_id=1, source_target_pairs={{0,2},{2,4},{4,6},{6,8},{8,10},{10,12},{12,14},{14,16},{16,18},{18... | collective-permute-start | bytes 9437192 | tf_op jit(solution)/shard_map/ppermute | solution.py:42
  501.8 1.6 copy-start.23
  503.4 39.4 %collective-permute-start.12 = (bf16[256,3,2048]{0,2,1:T(8,128)(2,1)S(1)}, bf16[256,3,2048]{0,2,1:T(8,128)(2,1)S(1)}, u32[]{:S(2)}, u32[]{:S(2)}) collective-permute-start(bf16[256,3,2048]{0,2,1:T(8,128)(2,1)S(1)} %collective-permute-done.11), channel_id=1, source_target_pairs={{0,2},{2,4},{4,6},{6,8},{8,10},{10,12},{12,14},{14,16},{16,18},{18... | collective-permute-start | bytes 9437192 | tf_op jit(solution)/shard_map/ppermute | solution.py:42
  542.8 1.6 copy-start.25
  544.4 39.5 %collective-permute-start.13 = (bf16[256,3,2048]{0,2,1:T(8,128)(2,1)S(1)}, bf16[256,3,2048]{0,2,1:T(8,128)(2,1)}, u32[]{:S(2)}, u32[]{:S(2)}) collective-permute-start(bf16[256,3,2048]{0,2,1:T(8,128)(2,1)S(1)} %collective-permute-done.12), channel_id=1, source_target_pairs={{0,2},{2,4},{4,6},{6,8},{8,10},{10,12},{12,14},{14,16},{16,18},{18... | collective-permute-start | bytes 9437192 | tf_op jit(solution)/shard_map/ppermute | solution.py:42
  583.9 76.2 %collective-permute-start.14 = (bf16[256,3,2048]{0,2,1:T(8,128)(2,1)}, bf16[256,3,2048]{0,2,1:T(8,128)(2,1)}, u32[]{:S(2)}, u32[]{:S(2)}) collective-permute-start(bf16[256,3,2048]{0,2,1:T(8,128)(2,1)} %collective-permute-done.13), channel_id=1, source_target_pairs={{0,2},{2,4},{4,6},{6,8},{8,10},{10,12},{12,14},{14,16},{16,18},{18... | collective-permute-start | bytes 9437192 | tf_op jit(solution)/shard_map/ppermute | solution.py:42
  585.5 0.7 copy-start.30
  586.2 0.6 copy-start.28
  642.1 9.4 copy-start.34
  651.6 16.5 %copy-start.26 = (bf16[256,3,2048]{0,2,1:T(8,128)(2,1)S(1)}, bf16[256,3,2048]{0,2,1:T(8,128)(2,1)}, u32[]{:S(2)}) copy-start(bf16[256,3,2048]{0,2,1:T(8,128)(2,1)} %copy-done.25) | copy-start | bytes 9437188
  660.2 9.9 copy-start.24
  660.2 11.8 copy-start.22
  664.1 9.7 copy-start.20
  668.1 7.6 copy-start.18
  670.0 7.6 copy-start.16
  671.9 7.6 copy-start.14
  673.8 7.7 copy-start.12
  675.7 7.7 copy-start.10
  677.6 7.7 copy-start.8
  679.6 7.7 copy-start.6
  681.5 7.7 copy-start.4
  683.4 7.7 copy-start.2
  800.8 2.6 copy-start.27
  804.6 2.1 collective-permute-start.15
  837.4 4.6 copy-start
  842.0 8.2 copy-start.29
  842.0 8.2 copy-start.31
  842.0 8.2 copy-start.32
  850.2 199.7 %copy-start.33 = (f32[128,16]{1,0:T(8,128)S(1)}, f32[128,16]{1,0:T(8,128)}, u32[]{:S(2)}) copy-start(f32[128,16]{1,0:T(8,128)} %get-tuple-element.342) | copy-start | bytes 24580
  1049.9 131.8 %reduce-scatter.2.cloned.1.call-start = ((), (), s32[]{:S(2)}) async-start(), calls=%async_computation.1 | async-start | bytes 6291456 | tf_op jit(solution)/shard_map/reduce_scatter | solution.py:100
  1076.3 32.7 %copy-start.35 = (f32[2048]{0:T(1024)S(1)}, f32[2048]{0:T(1024)}, u32[]{:S(2)}) copy-start(f32[2048]{0:T(1024)} %param.16) | copy-start | bytes 24580
Sparse Core Ops, SparseCore 0:
  1050.0 46.5 all-gather.3
  1128.2 53.4 reduce-scatter.1
